TPU v7x, 32 devices: a whole 2x2x4 slice. The times are simulated.
32 devices in a mesh: row: 8 (over z, y), col: 4 (over x, core).
Axes of the slice: x: 2, y: 2, z: 4, core: 2. Of those that a mesh axis runs over, the one named last changes fastest.
Arguments:
- trail_adjoint: float32 [4096, 4096], P('row', 'col'), may hold values from -6 to 6
- lower_new: float32 [4096, 256], P('row', 'col'), may hold values from -0.09375 to 0.09375
- upper_new: float32 [256, 4096], P('row', 'col'), may hold values from -0.09375 to 0.09375
- lower_old_top: float32 [256, 256], replicated, may hold values from -0.375 to 0.375
- lower_old: float32 [4096, 256], P('row', 'col'), may hold values from -0.09375 to 0.09375
- upper_old_left: float32 [256, 256], replicated, may hold values from -0.375 to 0.375
- upper_old: float32 [256, 4096], P('row', 'col'), may hold values from -0.09375 to 0.09375
- diag_lower_new: float32 [256, 256], replicated, as said below
- diag_upper_new: float32 [256, 256], replicated, as said below
- inverse_lower_new: float32 [256, 256], replicated, as said below
- inverse_upper_new: float32 [256, 256], replicated, as said below
- diag_lower_old: float32 [256, 256], replicated, as said below
- diag_upper_old: float32 [256, 256], replicated, as said below
- inverse_lower_old: float32 [256, 256], replicated, as said below
- inverse_upper_old: float32 [256, 256], replicated, as said below
Outputs:
- corner_old: float32 [256, 256], replicated
- strip_top: float32 [256, 256], replicated
- strip_bottom: float32 [4096, 256], P(('row', 'col'))
- band_left: float32 [256, 256], replicated
- band_right: float32 [256, 4096], P(None, 'col')
Inputs may be any that keep to these rules, and one draw needn't show every extreme that they name: `diag_lower_new`: unit lower triangular. `diag_upper_new`: upper triangular, diagonal from 1 to 2. `inverse_lower_new`: the inverse of diag_lower_new. `inverse_upper_new`: the inverse of diag_upper_new. `diag_lower_old`: unit lower triangular. `diag_upper_old`: upper triangular, diagonal from 1 to 2. `inverse_lower_old`: the inverse of diag_lower_old. `inverse_upper_old`: the inverse of diag_upper_old.
All inputs are finite; a program needn't handle non-finite values.
Results may differ from a plain program's by a relative error of at most 0.000075.
Values sent between devices are 32-bit elements; how exact they have to be, the bound alone decides.
A program may use at most 128 MiB of HBM per device.

v0:
```python
import jax
import jax.numpy as jnp
from jax import lax
from jax.sharding import PartitionSpec as P

precise = lax.Precision.HIGH


def dot(left, right, a, b):
    return lax.dot_general(left, right, (((a,), (b,)), ((), ())), precision=precise)


def body(an, ln, un, lot, lo, uol, uo, dln, dun, iln, iun, dlo, duo, ilo, iuo):
    width = iln.shape[0]
    uppers = lax.all_gather(jnp.concatenate((un[None], uo[None])), "row", axis=1, tiled=True)
    lowers = lax.all_gather(jnp.concatenate((ln[None], lo[None])), "col", axis=2, tiled=True)
    un, uo = (uppers[0], uppers[1])
    ln, lo = (lowers[0], lowers[1])
    mix_u = dot(dot(iuo, uol, 1, 0), iun, 1, 0)
    mix_l = dot(dot(iln, lot, 1, 0), ilo, 1, 0)
    ut = dot(iuo, uo, 1, 0) - dot(mix_u, un, 1, 0)
    lt = dot(lo, ilo, 1, 0) - dot(ln, mix_l, 1, 0)
    strip = -dot(an, ut, 1, 1)
    band = -dot(lt, an, 0, 0)
    left = -dot(band, un, 1, 1)
    both = -dot(jnp.concatenate((ln, lt), axis=1), strip, 0, 0)
    small = lax.psum(jnp.concatenate((left, both), axis=0), ("row", "col"))
    strip = lax.psum_scatter(strip, "col", scatter_dimension=0, tiled=True)
    band = lax.psum(band, "row")
    band_left = dot(small[:width], iun, 1, 1)
    strip_top = dot(iln, small[width : 2 * width], 0, 0)
    corner = small[2 * width :]
    return (corner, strip_top, strip, band_left, band)


def solution(mesh):
    split, whole = (P("row", "col"), P())
    return jax.shard_map(
        body,
        mesh=mesh,
        in_specs=(split, split, split, whole, split, whole, split) + (whole,) * 8,
        out_specs=(P(), P(), P(("row", "col"), None), P(), P(None, "col")),
        check_vma=False,
    )
```

profile of v0, /device:TPU:0, one launch (start us, length us, event | category | flops | bytes accessed | tf_op | source)
XLA Modules:
  0.0 331.9 jit_solution(3750939363003081247)
XLA Ops:
  7.3 1.8 pad_maximum_fusion.1
  9.1 0.0 all-gather.5.cloned.1.call-start
  9.2 1.7 pad_maximum_fusion.2
  10.9 0.0 all-reduce.3.cloned.1.call-start
  10.9 1.3 fusion.10
  12.3 0.3 fusion.11
  12.6 0.3 fusion.12
  12.9 1.0 fusion.13
  13.8 15.8 %all-gather.3.cloned.1.call-done = f32[2,512,256]{1,2,0:T(8,128)} async-done(((f32[2,512,64]{1,2,0:T(8,128)}), f32[2,512,256]{1,2,0:T(8,128)}) %all-gather.3.cloned.1.call-update) | async-done | bytes 1048592 | tf_op jit(solution)/shard_map/all_gather | solution.py:16
  29.6 2.0 slice_bitcast_fusion.5
  31.6 1.5 fusion.5
  33.1 0.5 convolution_subtract_fusion
  33.5 0.8 copy-done.2
  34.3 1.1 convolution_negate_fusion
  35.4 46.1 %all-gather.5.cloned.1.call-done = f32[2,256,1024]{2,1,0:T(8,128)} async-done(((f32[2,32,1024]{2,1,0:T(8,128)}), f32[2,256,1024]{2,1,0:T(8,128)}) %all-gather.5.cloned.1.call-update) | async-done | bytes 2097168 | tf_op jit(solution)/shard_map/all_gather | solution.py:15
  81.5 2.5 fusion.4
  84.0 1.0 fusion
  85.0 1.9 convolution_negate_fusion.2
  87.0 0.6 convolution_negate_fusion.1
  87.6 0.7 convolution_negate_fusion.3
  88.3 0.9 pad_maximum_fusion
  89.3 0.5 reduce-scatter.2.cloned.1.call-update
  89.9 0.5 all-reduce.5.cloned.1.call-update
  90.5 127.4 %all-reduce.3.cloned.1.call-done = f32[768,256]{1,0:T(8,128)} async-done(((f32[768,256]{1,0:T(8,128)}), f32[768,256]{1,0:T(8,128)}) %all-reduce.3.cloned.1.call-update) | async-done | bytes 786448 | tf_op jit(solution)/shard_map/psum | solution.py:27
  217.9 1.3 convolution_bitcast_fusion.1
  219.2 0.8 copy.16
  220.1 1.7 slice.32
  221.7 2.0 fusion.6
  223.7 17.2 %reduce-scatter.2.cloned.1.call-done = f32[128,256]{0,1:T(8,128)} async-done(((f32[512,256]{0,1:T(8,128)}), f32[128,256]{0,1:T(8,128)}) %reduce-scatter.2.cloned.1.call-update) | async-done | bytes 131088 | tf_op jit(solution)/shard_map/reduce_scatter | solution.py:28
  240.9 1.7 copy.17
  242.6 80.5 %all-reduce.5.cloned.1.call-done = f32[256,1024]{1,0:T(8,128)} async-done(((f32[256,1024]{1,0:T(8,128)}), f32[256,1024]{1,0:T(8,128)}) %all-reduce.5.cloned.1.call-update) | async-done | bytes 1048592 | tf_op jit(solution)/shard_map/psum | solution.py:29
  323.1 2.3 copy.20
  (33 shorter events, 0.2 us)
Async XLA Ops:
  7.2 27.2 %copy-start = (f32[512,1024]{1,0:T(8,128)S(1)}, f32[512,1024]{1,0:T(8,128)}, u32[]{:S(2)}) copy-start(f32[512,1024]{1,0:T(8,128)} %param.15) | copy-start | bytes 6291460
  7.2 5.1 %copy-start.8 = (f32[256,256]{1,0:T(8,128)S(1)}, f32[256,256]{1,0:T(8,128)}, u32[]{:S(2)}) copy-start(f32[256,256]{1,0:T(8,128)} %param.24) | copy-start | bytes 786436
  7.2 5.4 %copy-start.11 = (f32[256,256]{1,0:T(8,128)S(1)}, f32[256,256]{1,0:T(8,128)}, u32[]{:S(2)}) copy-start(f32[256,256]{1,0:T(8,128)} %param.25) | copy-start | bytes 786436
  7.2 5.4 %copy-start.13 = (f32[256,256]{1,0:T(8,128)S(1)}, f32[256,256]{1,0:T(8,128)}, u32[]{:S(2)}) copy-start(f32[256,256]{1,0:T(8,128)} %param.20) | copy-start | bytes 786436
  7.2 5.6 %copy-start.10 = (f32[256,256]{1,0:T(8,128)S(1)}, f32[256,256]{1,0:T(8,128)}, u32[]{:S(2)}) copy-start(f32[256,256]{1,0:T(8,128)} %param.23) | copy-start | bytes 786436
  7.2 22.4 %all-gather.3.cloned.1.call-start = ((), (), s32[]{:S(2)}) async-start(), calls=%async_computation.1 | async-start | bytes 1310720 | tf_op jit(solution)/shard_map/all_gather | solution.py:16
  9.1 72.4 %all-gather.5.cloned.1.call-start = ((), (), s32[]{:S(2)}) async-start(), calls=%async_computation.2 | async-start | bytes 2359296 | tf_op jit(solution)/shard_map/all_gather | solution.py:15
  10.9 207.0 %all-reduce.3.cloned.1.call-start = ((), (), s32[]{:S(2)}) async-start(), calls=%async_computation.3 | async-start | bytes 1572864 | tf_op jit(solution)/shard_map/psum | solution.py:27
  29.6 3.4 %copy-start.6 = (f32[2,512,256]{1,2,0:T(8,128)S(1)}, f32[2,512,256]{1,2,0:T(8,128)}, u32[]{:S(2)}) copy-start(f32[2,512,256]{1,2,0:T(8,128)} %all-gather.3.cloned.1.call-done) | copy-start | bytes 3145732
  33.5 0.8 copy-start.2
  35.4 52.2 %copy-start.1 = (f32[256,1024]{1,0:T(8,128)}, f32[256,1024]{1,0:T(8,128)S(1)}, u32[]{:S(2)}) copy-start(f32[256,1024]{1,0:T(8,128)S(1)} %convolution_negate_fusion) | copy-start | bytes 3145732
  81.5 2.5 copy-start.4
  81.5 2.5 copy-start.12
  85.0 2.0 copy-start.3
  85.0 2.0 copy-start.7
  87.0 1.3 copy-start.5
  88.3 129.6 %copy-start.9 = (f32[256,256]{1,0:T(8,128)S(1)}, f32[256,256]{1,0:T(8,128)}, u32[]{:S(2)}) copy-start(f32[256,256]{1,0:T(8,128)} %param.22) | copy-start | bytes 786436
  89.3 151.6 %reduce-scatter.2.cloned.1.call-start = ((), (), s32[]{:S(2)}) async-start(), calls=%async_computation.4 | async-start | bytes 655360 | tf_op jit(solution)/shard_map/reduce_scatter | solution.py:28
  89.9 233.2 %all-reduce.5.cloned.1.call-start = ((), (), s32[]{:S(2)}) async-start(), calls=%async_computation.5 | async-start | bytes 2097152 | tf_op jit(solution)/shard_map/psum | solution.py:29
Sparse Core Ops, SparseCore 0:
  10.2 19.4 all-gather.2
  32.4 49.0 all-gather.4
  89.4 128.4 all-reduce.2
  220.2 20.6 reduce-scatter.1
  244.8 78.1 all-reduce.4
where the time goes:
time: 332 us
  waiting for transfers between devices  288 us (87%)
  matrix products  15.8 us (5%)
  between operations  14 us (4%)
  local copies, waits for them, and re-layouts  9.28 us (3%)
  other arithmetic  4.48 us (1%)
    psum x1, waiting for transfers between devices, body(): small = lax.psum(jnp.concatenate((left, both), axis=0), ('row', 'col'))  127 us
    psum x1, waiting for transfers between devices, body(): band = lax.psum(band, 'row')  80.5 us
    all_gather x1, waiting for transfers between devices, body(): lax.all_gather(jnp.concatenate((un[None], uo[None])), 'row', axis=1, tile...  46.1 us
    reduce_scatter x1, waiting for transfers between devices, body(): strip = lax.psum_scatter(strip, 'col', scatter_dimension=0, tiled=True)  17.2 us
    dot_general x14, matrix products, dot(): lax.dot_general(left, right, (((a,), (b,)), ((), ())), precision=precise)  15.8 us
    all_gather x1, waiting for transfers between devices, body(): lax.all_gather(jnp.concatenate((ln[None], lo[None])), 'col', axis=2, tile...  15.8 us
  transfers between devices with their start and end apart: 5, of which 5 were waited for; matrix products, arithmetic and copies ran while one was open for 5% of the time, Pallas kernels for 0%

commit v1 on v0

--- a/solution.py
+++ b/solution.py
@@ -26,7 +26,8 @@
     both = -dot(jnp.concatenate((ln, lt), axis=1), strip, 0, 0)
     small = lax.psum(jnp.concatenate((left, both), axis=0), ("row", "col"))
     strip = lax.psum_scatter(strip, "col", scatter_dimension=0, tiled=True)
-    band = lax.psum(band, "row")
+    parts = lax.all_gather(band, "row")
+    band = jnp.sum(parts, axis=0)
     band_left = dot(small[:width], iun, 1, 1)
     strip_top = dot(iln, small[width : 2 * width], 0, 0)
     corner = small[2 * width :]

time: 332 us -> 380 us (1.14)
  waiting for transfers between devices: 288 us -> 333 us
  other arithmetic: 4.48 us -> 9.8 us
    all_gather x0 -> x1, waiting for transfers between devices: none -> 125 us  [body(): parts = lax.all_gather(band, 'row')]
    psum x1 -> x0, waiting for transfers between devices: 80.5 us -> none  [body(): band = lax.psum(band, 'row')]
    reduce_sum x0 -> x1, other arithmetic: none -> 5.35 us  [body(): band = jnp.sum(parts, axis=0)]
  transfers between devices with their start and end apart: 5 -> 5, of which waited for: 5 -> 5; matrix products, arithmetic and copies ran while one was open for 5% -> 4% of each run, Pallas kernels for 0% -> 0%
where the time goes in v1:
time: 380 us
  waiting for transfers between devices  333 us (88%)
  matrix products  15.8 us (4%)
  between operations  14 us (4%)
  other arithmetic  9.8 us (3%)
  local copies, waits for them, and re-layouts  6.97 us (2%)
    psum x1, waiting for transfers between devices, body(): small = lax.psum(jnp.concatenate((left, both), axis=0), ('row', 'col'))  127 us
    all_gather x1, waiting for transfers between devices, body(): parts = lax.all_gather(band, 'row')  125 us
    all_gather x1, waiting for transfers between devices, body(): lax.all_gather(jnp.concatenate((un[None], uo[None])), 'row', axis=1, tile...  46.1 us
    reduce_scatter x1, waiting for transfers between devices, body(): strip = lax.psum_scatter(strip, 'col', scatter_dimension=0, tiled=True)  17.2 us
    dot_general x14, matrix products, dot(): lax.dot_general(left, right, (((a,), (b,)), ((), ())), precision=precise)  15.8 us
    all_gather x1, waiting for transfers between devices, body(): lax.all_gather(jnp.concatenate((ln[None], lo[None])), 'col', axis=2, tile...  15.8 us
  transfers between devices with their start and end apart: 5, of which 5 were waited for; matrix products, arithmetic and copies ran while one was open for 4% of the time, Pallas kernels for 0%

profile of v1, /device:TPU:0, one launch (start us, length us, event | category | flops | bytes accessed | tf_op | source)
XLA Modules:
  0.0 379.8 jit_solution(1093901752198425080)
XLA Ops:
  7.3 1.8 pad_maximum_fusion.1
  9.1 0.0 all-gather.7.cloned.1.call-start
  9.2 1.7 pad_maximum_fusion.2
  10.9 0.0 all-reduce.2.cloned.1.call-start
  10.9 1.3 fusion.10
  12.3 0.3 fusion.11
  12.6 0.3 fusion.12
  12.9 1.0 fusion.13
  13.8 15.8 %all-gather.5.cloned.1.call-done = f32[2,512,256]{1,2,0:T(8,128)} async-done(((f32[2,512,64]{1,2,0:T(8,128)}), f32[2,512,256]{1,2,0:T(8,128)}) %all-gather.5.cloned.1.call-update) | async-done | bytes 1048592 | tf_op jit(solution)/shard_map/all_gather | solution.py:16
  29.6 2.0 slice_bitcast_fusion.5
  31.6 1.5 fusion.5
  33.1 0.5 convolution_subtract_fusion
  33.5 0.8 copy-done.2
  34.3 1.1 convolution_negate_fusion
  35.4 46.1 %all-gather.7.cloned.1.call-done = f32[2,256,1024]{2,1,0:T(8,128)} async-done(((f32[2,32,1024]{2,1,0:T(8,128)}), f32[2,256,1024]{2,1,0:T(8,128)}) %all-gather.7.cloned.1.call-update) | async-done | bytes 2097168 | tf_op jit(solution)/shard_map/all_gather | solution.py:15
  81.5 2.5 fusion.4
  84.0 1.0 fusion
  85.0 1.9 convolution_negate_fusion.2
  87.0 0.6 convolution_negate_fusion.1
  87.6 0.7 convolution_negate_fusion.3
  88.3 0.9 pad_maximum_fusion
  89.3 0.5 reduce-scatter.2.cloned.1.call-update
  89.9 0.5 all-gather.9.cloned.1.call-update
  90.4 127.4 %all-reduce.2.cloned.1.call-done = f32[768,256]{1,0:T(8,128)} async-done(((f32[768,256]{1,0:T(8,128)}), f32[768,256]{1,0:T(8,128)}) %all-reduce.2.cloned.1.call-update) | async-done | bytes 786448 | tf_op jit(solution)/shard_map/psum | solution.py:27
  217.9 1.3 convolution_bitcast_fusion.1
  219.2 0.8 copy.16
  220.0 1.7 slice.32
  221.7 2.0 fusion.6
  223.7 17.2 %reduce-scatter.2.cloned.1.call-done = f32[128,256]{0,1:T(8,128)} async-done(((f32[512,256]{0,1:T(8,128)}), f32[128,256]{0,1:T(8,128)}) %reduce-scatter.2.cloned.1.call-update) | async-done | bytes 131088 | tf_op jit(solution)/shard_map/reduce_scatter | solution.py:28
  240.9 1.7 copy.17
  242.5 125.4 %all-gather.9.cloned.1.call-done = f32[2048,1024]{1,0:T(8,128)} async-done(((f32[256,1024]{1,0:T(8,128)}), f32[2048,1024]{1,0:T(8,128)}) %all-gather.9.cloned.1.call-update) | async-done | bytes 8388624 | tf_op jit(solution)/shard_map/all_gather | solution.py:29
  368.0 5.3 %reduce_sum.9 = f32[256,1024]{1,0:T(8,128)} reduce(f32[8,256,1024]{2,1,0:T(8,128)} %bitcast.45, f32[]{:T(128)} %constant.0.clone.1), dimensions={0}, to_apply=%region_2.0 | reduce | flops 1835008 | bytes 9437188 | tf_op jit(solution)/shard_map/reduce_sum | solution.py:30
  (33 shorter events, 0.2 us)
Async XLA Ops:
  7.2 27.2 %copy-start = (f32[512,1024]{1,0:T(8,128)S(1)}, f32[512,1024]{1,0:T(8,128)}, u32[]{:S(2)}) copy-start(f32[512,1024]{1,0:T(8,128)} %param.15) | copy-start | bytes 6291460
  7.2 5.1 %copy-start.8 = (f32[256,256]{1,0:T(8,128)S(1)}, f32[256,256]{1,0:T(8,128)}, u32[]{:S(2)}) copy-start(f32[256,256]{1,0:T(8,128)} %param.24) | copy-start | bytes 786436
  7.2 5.4 %copy-start.11 = (f32[256,256]{1,0:T(8,128)S(1)}, f32[256,256]{1,0:T(8,128)}, u32[]{:S(2)}) copy-start(f32[256,256]{1,0:T(8,128)} %param.25) | copy-start | bytes 786436
  7.2 5.4 %copy-start.13 = (f32[256,256]{1,0:T(8,128)S(1)}, f32[256,256]{1,0:T(8,128)}, u32[]{:S(2)}) copy-start(f32[256,256]{1,0:T(8,128)} %param.20) | copy-start | bytes 786436
  7.2 5.6 %copy-start.10 = (f32[256,256]{1,0:T(8,128)S(1)}, f32[256,256]{1,0:T(8,128)}, u32[]{:S(2)}) copy-start(f32[256,256]{1,0:T(8,128)} %param.23) | copy-start | bytes 786436
  7.2 22.4 %all-gather.5.cloned.1.call-start = ((), (), s32[]{:S(2)}) async-start(), calls=%async_computation.1 | async-start | bytes 1310720 | tf_op jit(solution)/shard_map/all_gather | solution.py:16
  9.1 72.4 %all-gather.7.cloned.1.call-start = ((), (), s32[]{:S(2)}) async-start(), calls=%async_computation.2 | async-start | bytes 2359296 | tf_op jit(solution)/shard_map/all_gather | solution.py:15
  10.9 207.0 %all-reduce.2.cloned.1.call-start = ((), (), s32[]{:S(2)}) async-start(), calls=%async_computation.3 | async-start | bytes 1572864 | tf_op jit(solution)/shard_map/psum | solution.py:27
  29.6 3.4 copy-start.6
  33.5 0.8 copy-start.2
  35.4 52.2 %copy-start.1 = (f32[256,1024]{1,0:T(8,128)}, f32[256,1024]{1,0:T(8,128)S(1)}, u32[]{:S(2)}) copy-start(f32[256,1024]{1,0:T(8,128)S(1)} %convolution_negate_fusion) | copy-start | bytes 3145732
  81.5 2.5 copy-start.4
  81.5 2.5 copy-start.12
  85.0 2.0 copy-start.3
  85.0 2.0 copy-start.7
  87.0 1.3 copy-start.5
  88.3 129.5 %copy-start.9 = (f32[256,256]{1,0:T(8,128)S(1)}, f32[256,256]{1,0:T(8,128)}, u32[]{:S(2)}) copy-start(f32[256,256]{1,0:T(8,128)} %param.22) | copy-start | bytes 786436
  89.3 151.6 %reduce-scatter.2.cloned.1.call-start = ((), (), s32[]{:S(2)}) async-start(), calls=%async_computation.4 | async-start | bytes 655360 | tf_op jit(solution)/shard_map/reduce_scatter | solution.py:28
  89.9 278.1 %all-gather.9.cloned.1.call-start = ((), (), s32[]{:S(2)}) async-start(), calls=%async_computation.5 | async-start | bytes 9437184 | tf_op jit(solution)/shard_map/all_gather | solution.py:29
Sparse Core Ops, SparseCore 0:
  10.2 19.4 all-gather.4
  32.4 49.0 all-gather.6
  89.4 128.4 all-reduce.1
  220.2 20.6 reduce-scatter.1
  243.4 124.4 all-gather.8
